TPU v7x, 256 devices: a whole 4x4x8 slice. The times are simulated.
256 devices in a mesh: kx: 8 (over z), ht: 8 (over y, core), real: 4 (over x).
Axes of the slice: x: 4, y: 4, z: 8, core: 2. Of those that a mesh axis runs over, the one named last changes fastest.
Arguments:
- velocity: float32 [3, 4, 32, 512, 128], P(None, 'real', 'kx', 'ht'), may hold values from -6 to 6
- low_index: int32 [8], replicated, may hold values from 0 to 31, as said below
- neighbours: int32 [32, 8], P('kx'), may hold values from 0 to 31, as said below
- owner_map: int32 [64], replicated, may hold values from 0 to 63, each once
- mode_counts: int32 [32], P('kx'), may hold values from 16 to 64
- helmholtz: float32 [64, 512, 512], P(('kx', 'ht')), may hold values from -0.25 to 0.25
Outputs:
- velocity_next: float32 [3, 4, 32, 512, 128], P(None, 'real', 'kx', 'ht')
Inputs may be any that keep to these rules, and one draw needn't show every extreme that they name: `low_index`: distinct values. neighbours[m, j] lies within 4 modes of m, counting circularly over the 32 modes; offsets of + 4 and - 4 both occur.
All inputs are finite; a program needn't handle non-finite values.
Results may differ from a plain program's by a relative error of at most 0.0001.
Values sent between devices are 32-bit elements; how exact they have to be, the bound alone decides.
A program may use at most 64 MiB of HBM per device.

v0:
```python
import jax
import jax.numpy as jnp
from jax import lax
from jax.sharding import PartitionSpec as P

dt_step = 0.1


def extended_2(block, sides, width):
    for axis, dim in sides:
        count = lax.axis_size(axis)
        forward = [(i, i + 1) for i in range(count - 1)]
        forward.append((count - 1, 0))
        backward = [(target, source) for source, target in forward]
        low = lax.ppermute(
            lax.slice_in_dim(block, block.shape[dim] - width, None, axis=dim), axis, forward
        )
        high = lax.ppermute(lax.slice_in_dim(block, 0, width, axis=dim), axis, backward)
        block = jnp.concatenate([low, block, high], axis=dim)
    return block


def spanwise_tables(mode_count, point_count):
    column_ids = jnp.arange(2 * mode_count)
    wavenumber = (column_ids // 2).astype(jnp.float32)
    imag_part = column_ids % 2
    positions = 2.0 * jnp.pi * jnp.arange(point_count).astype(jnp.float32) / point_count
    phases = wavenumber[:, None] * positions[None, :]
    forward = jnp.where(imag_part[:, None] == 0, jnp.cos(phases), -jnp.sin(phases)) / jnp.sqrt(
        jnp.float32(mode_count)
    )
    backward = forward.T * (2.0 * mode_count / point_count)
    return (forward, backward)


def apply_inverse(block, helmholtz, kx_count, ht_count, slots_dev, rows_ht):
    components, reals_dev, band_modes = (block.shape[0], block.shape[1], block.shape[2])
    regrouped = block.reshape(
        components, reals_dev, band_modes, kx_count, ht_count, slots_dev, 2, rows_ht
    )
    regrouped = regrouped.transpose(0, 1, 3, 2, 5, 6, 4, 7)
    regrouped = regrouped.reshape(
        components, reals_dev, kx_count * band_modes, slots_dev, 2, ht_count * rows_ht
    )
    solved = jnp.einsum("syx,crmspx->crmspy", helmholtz, regrouped, precision=lax.Precision.HIGHEST)
    solved = solved.reshape(
        components, reals_dev, kx_count, band_modes, slots_dev, 2, ht_count, rows_ht
    )
    solved = solved.transpose(0, 1, 3, 2, 6, 4, 5, 7)
    return solved.reshape(block.shape)


def local(velocity, low_index, neighbours, owner_map, mode_counts, helmholtz):
    highest = lax.Precision.HIGHEST
    components, reals_dev, band_modes, rows_ht, columns = velocity.shape
    kz_modes = columns // 2
    forward, backward = spanwise_tables(kz_modes, 4 * kz_modes)
    kx_count = lax.axis_size("kx")
    ht_count = lax.axis_size("ht")
    kx_total = band_modes * kx_count
    realizations = reals_dev * lax.axis_size("real")
    owners = kx_count * ht_count
    slots_dev = kz_modes // owners
    width_out = slots_dev * 2 * rows_ht
    low_members = low_index.shape[0]
    band_start = lax.axis_index("kx") * band_modes
    global_modes = band_start + jnp.arange(band_modes, dtype=jnp.int32)
    low_select = (low_index[:, None] == global_modes[None, :]).astype(jnp.float32)
    high_mask = 1.0 - jnp.sum(low_select, axis=0)
    offsets = (neighbours - global_modes[:, None] + kx_total // 2) % kx_total - kx_total // 2
    local_partner = jnp.arange(band_modes, dtype=jnp.int32)[:, None] + band_modes + offsets
    column_mask = ((jnp.arange(columns) // 2)[None, :] < mode_counts[:, None]).astype(jnp.float32)
    inverse_map = (
        jnp.zeros((kz_modes,), jnp.int32).at[owner_map].set(jnp.arange(kz_modes, dtype=jnp.int32))
    )
    current = velocity
    physical = jnp.dot(current, forward, precision=highest)
    extended = extended_2(physical, (("kx", 2),), band_modes)
    own_low = jnp.einsum("jm,crmyz->crjyz", low_select, physical, precision=highest)
    low_fields = lax.psum(own_low, "kx")
    high_low = jnp.zeros_like(physical)
    stresses = []
    for member in range(low_members):
        partner = jnp.take(extended, local_partner[:, member], axis=2)
        low_one = low_fields[:, :, member : member + 1]
        high_low = high_low + low_one * partner[1:2] + partner * low_one[1:2]
        weighted = physical * (partner[1:2] * high_mask[None, None, :, None, None])
        stresses.append(jnp.sum(weighted, axis=(1, 2)))
    stress = jnp.stack(stresses, axis=1)
    nonlinear = jnp.dot(high_low, backward, precision=highest)
    summed = lax.psum(stress, ("kx", "real"))
    low_forcing = jnp.dot(summed / realizations, backward, precision=highest)
    forcing = nonlinear * high_mask[None, None, :, None, None]
    forcing = (
        forcing + jnp.einsum("jm,cjyk->cmyk", low_select, low_forcing, precision=highest)[:, None]
    )
    forcing = forcing * column_mask[None, None, :, None, :]
    updated = current + dt_step * forcing
    slotted = jnp.take(
        updated.reshape(components, reals_dev, band_modes, rows_ht, kz_modes, 2), owner_map, axis=4
    )
    outgoing = slotted.reshape(components, reals_dev, band_modes, rows_ht, owners, slots_dev, 2)
    outgoing = outgoing.transpose(0, 1, 2, 4, 5, 6, 3)
    flat_out = outgoing.reshape(components, reals_dev, band_modes, owners, width_out)
    applied = apply_inverse(
        lax.all_to_all(flat_out, ("kx", "ht"), split_axis=3, concat_axis=3, tiled=True),
        helmholtz,
        kx_count,
        ht_count,
        slots_dev,
        rows_ht,
    )
    returned = lax.all_to_all(applied, ("kx", "ht"), split_axis=3, concat_axis=3, tiled=True)
    restored = returned.reshape(components, reals_dev, band_modes, owners, slots_dev, 2, rows_ht)
    restored = restored.transpose(0, 1, 2, 6, 3, 4, 5).reshape(
        components, reals_dev, band_modes, rows_ht, kz_modes, 2
    )
    current = jnp.take(restored, inverse_map, axis=4).reshape(
        components, reals_dev, band_modes, rows_ht, columns
    )
    return current


def solution(mesh):
    in_specs = (
        P(None, "real", "kx", "ht", None),
        P(),
        P("kx", None),
        P(),
        P("kx"),
        P(("kx", "ht"), None, None),
    )
    out_specs = P(None, "real", "kx", "ht", None)
    return jax.shard_map(local, mesh=mesh, in_specs=in_specs, out_specs=out_specs, check_vma=False)
```

profile of v0, /device:TPU:1, one launch (start us, length us, event | category | flops | bytes accessed | tf_op | source)
XLA Modules:
  0.0 327.1 jit_solution(15920989410416831472)
XLA Ops:
  6.6 2.4 fusion.12
  9.0 2.5 collective-permute-start
  11.5 4.0 %collective-permute-start.1 = (f32[3,1,4,64,256]{4,3,2,0,1:T(8,128)S(1)}, f32[3,1,4,64,256]{4,3,2,0,1:T(8,128)}, u32[]{:S(2)}, u32[]{:S(2)}) collective-permute-start(f32[3,1,4,64,256]{4,3,2,0,1:T(8,128)S(1)} %bitcast.259), channel_id=1, source_target_pairs={{32,0},{64,32},{96,64},{128,96},{160,128},{192,160},{224,192},{0,2... | collective-permute-start | bytes 2359304 | tf_op jit(solution)/shard_map/ppermute | solution.py:18
  15.6 3.1 convolution_bitcast_fusion
  19.8 12.9 %collective-permute-done = f32[3,1,4,64,256]{4,3,2,0,1:T(8,128)S(1)} collective-permute-done((f32[3,1,4,64,256]{4,3,2,0,1:T(8,128)S(1)}, f32[3,1,4,64,256]{4,3,2,0,1:T(8,128)S(1)}, u32[]{:S(2)}, u32[]{:S(2)}) %collective-permute-start) | collective-permute-done | bytes 786464 | tf_op jit(solution)/shard_map/ppermute | solution.py:15
  33.6 1.8 maximum_bitcast_fusion
  35.4 1.6 gather_fusion.7
  37.0 1.5 gather_fusion.5
  38.5 1.5 gather_fusion.4
  40.0 1.5 gather_fusion.3
  41.5 1.5 gather_fusion.2
  43.0 1.5 gather_fusion.1
  44.5 1.5 gather_fusion
  46.0 1.5 gather_fusion.6
  47.5 1.4 bitcast_select_fusion.2
  48.9 1.3 bitcast_select_fusion.4
  52.1 1.4 multiply_bitcast_fusion.1
  55.4 3.9 %stack.35 = f32[3,8,64,256]{3,1,2,0:T(8,128)} concatenate(f32[3,1,64,256]{3,1,2,0:T(1,128)S(1)} %stack.27, f32[3,1,64,256]{3,1,2,0:T(1,128)S(1)} %stack.28, f32[3,1,64,256]{3,1,2,0:T(1,128)S(1)} %stack.29, f32[3,1,64,256]{3,1,2,0:T(1,128)S(1)} %stack.30, f32[3,1,64,256]{3,1,2,0:T(1,128)S(1)} %stack.31, f32[3,1,64,256]{3,1,2,0:T(1,128)S(1)} %stack.32, ...), dimensions={1} | concatenate | bytes 3145728 | tf_op jit(solution)/shard_map/stack | solution.py:89
  60.4 35.1 %all-reduce.3.cloned.1.call-done = f32[3,1,8,64,256]{4,2,3,0,1:T(8,128)} async-done(((f32[3,1,8,64,256]{4,2,3,0,1:T(8,128)}), f32[3,1,8,64,256]{4,2,3,0,1:T(8,128)}) %all-reduce.3.cloned.1.call-update) | async-done | bytes 1572880 | tf_op jit(solution)/shard_map/psum | solution.py:80
  95.5 7.7 %fusion.51 = (f32[3,1,1,64,256]{4,2,3,0,1:T(1,128)S(1)}, f32[3,1,1,64,256]{4,2,3,0,1:T(1,128)S(1)}, f32[3,1,1,64,256]{4,2,3,0,1:T(1,128)S(1)}, f32[3,1,1,64,256]...) fusion(f32[3,1,8,64,256]{4,2,3,0,1:T(8,128)} %all-reduce.3.clon, ...), kind=kLoop, calls=%fused_computation.172 | loop fusion | bytes 3145728 | tf_op jit(solution)/shard_map/slice | solution.py:85
  108.7 3.5 %fusion.52 = (f32[1,1,1,64,256]{4,2,3,0,1:T(1,128)S(1)}, f32[1,1,1,64,256]{4,2,3,0,1:T(1,128)S(1)}, f32[1,1,1,64,256]{4,2,3,0,1:T(1,128)S(1)}, f32[1,1,1,64,256]...) fusion(f32[3,1,8,64,256]{4,2,3,0,1:T(8,128)} %all-reduce.3.clon, ...), kind=kLoop, calls=%fused_computation.173 | loop fusion | bytes 1048576 | tf_op jit(solution)/shard_map/slice | solution.py:86
  116.0 133.7 %all-reduce.5.cloned.1.call-done = f32[3,8,64,256]{3,1,2,0:T(8,128)} async-done(((f32[3,8,64,256]{3,1,2,0:T(8,128)}), f32[3,8,64,256]{3,1,2,0:T(8,128)}) %all-reduce.5.cloned.1.call-update) | async-done | bytes 1572880 | tf_op jit(solution)/shard_map/psum | solution.py:91
  249.7 3.5 %fusion = f32[3,8,64,128]{3,1,2,0:T(8,128)S(1)} fusion(f32[3,8,64,256]{3,1,2,0:T(8,128)} %all-reduce.5.cloned.1.call-done, f32[256]{0:T(256)S(1)} %convert_multiply_fusion, f32[128]{0:T(128)} %copy-done.17, pred[128]{0:T(512)(128)(4,1)S(1)} %fusion.42), kind=kOutput, calls=%fused_computation.12 | convolution fusion | flops 604504064 | bytes 2360960 | tf_op jit(solution)/shard_map/dot_general | solution.py:92
  253.2 1.2 fusion.50
  254.4 5.9 %fusion.6 = f32[3,1,4,64,128]{4,3,2,0,1:T(8,128)} fusion(f32[3,1,4,64,128]{4,3,2,1,0:T(8,128)S(1)} %copy-done.14, f32[3,64,128,4]{2,3,1,0:T(4,128)S(1)} %fusion.50, f32[4,128]{1,0:T(4,128)S(1)} %compare_convert_fusion.1, f32[4]{0:T(128)} %copy-done.27, f32[256]{0:T(256)S(1)} %convert_multiply_fusion, f32[128]{0:T(128)} %copy-done.17, ...), kind=kOutput, calls=%fused_computation.21 | convolution fusion | flops 310280192 | bytes 11669168 | tf_op jit(solution)/shard_map/dot_general | solution.py:90
  260.3 1.3 copy.38
  264.4 27.5 %all_to_all.10 = f32[3,1,4,64,128]{4,2,0,1,3:T(4,128)S(1)} all-to-all(f32[3,1,4,64,128]{4,2,0,1,3:T(4,128)S(1)} %reshape.457), channel_id=1, replica_groups=mesh['kx'=8,'ht'=8,'real'=4] {'kx','ht'}, dimensions={3} | all-to-all | bytes 786432 | tf_op jit(solution)/shard_map/all_to_all | solution.py:106
  292.8 1.5 convolution_bitcast_fusion.1
  294.9 1.3 reshape.459
  296.2 5.5 %all-to-all-start.1 = ((f32[3,1,4,64,128]{4,2,0,1,3:T(4,128)}), f32[3,1,4,64,128]{4,2,0,1,3:T(4,128)S(1)}, u32[]{:S(2)}, u32[]{:S(2)}) async-start(f32[3,1,4,64,128]{4,2,0,1,3:T(4,128)} %reshape.459), calls=%async_computation.1 | async-start | bytes 786432 | tf_op jit(solution)/shard_map/all_to_all | solution.py:113
  302.6 14.2 %all-to-all-done.1 = f32[3,1,4,64,128]{4,2,0,1,3:T(4,128)S(1)} async-done(((f32[3,1,4,64,128]{4,2,0,1,3:T(4,128)}), f32[3,1,4,64,128]{4,2,0,1,3:T(4,128)S(1)}, u32[]{:S(2)}, u32[]{:S(2)}) %all-to-all-start.1) | async-done | bytes 393248 | tf_op jit(solution)/shard_map/all_to_all | solution.py:113
  317.5 1.1 gather_fusion.9
  (161 shorter events, 23.1 us)
Async XLA Ops:
  6.5 286.2 %copy-start = (f32[1,512,512]{2,1,0:T(8,128)S(1)}, f32[1,512,512]{2,1,0:T(8,128)}, u32[]{:S(2)}) copy-start(f32[1,512,512]{2,1,0:T(8,128)} %param.15) | copy-start | bytes 3145732
  6.5 89.0 %all-reduce.3.cloned.1.call-start = ((), (), s32[]{:S(2)}) async-start(), calls=%async_computation.2 | async-start | bytes 3145728 | tf_op jit(solution)/shard_map/psum | solution.py:80
  6.6 12.2 %copy-start.17 = (f32[128]{0:T(128)}, f32[128]{0:T(128)S(1)}, u32[]{:S(2)}) copy-start(f32[128]{0:T(128)S(1)} %fusion.45) | copy-start | bytes 1540
  6.6 12.2 %copy-start.28 = (s32[4,8]{1,0:T(4,128)S(1)}, s32[4,8]{1,0:T(4,128)}, u32[]{:S(2)}) copy-start(s32[4,8]{1,0:T(4,128)} %param.12) | copy-start | bytes 388
  6.6 13.0 %copy-start.29 = (s32[8]{0:T(128)S(1)}, s32[8]{0:T(128)}, u32[]{:S(2)}) copy-start(s32[8]{0:T(128)} %param.11) | copy-start | bytes 100
  9.0 23.7 %copy-start.1 = (f32[256,3,4,64]{0,3,2,1:T(8,128)}, f32[256,3,4,64]{0,3,2,1:T(8,128)S(1)}, u32[]{:S(2)}) copy-start(f32[256,3,4,64]{0,3,2,1:T(8,128)S(1)} %fusion.12) | copy-start | bytes 2359300
  9.0 23.7 %collective-permute-start = (f32[3,1,4,64,256]{4,3,2,0,1:T(8,128)S(1)}, f32[3,1,4,64,256]{4,3,2,0,1:T(8,128)S(1)}, u32[]{:S(2)}, u32[]{:S(2)}) collective-permute-start(f32[3,1,4,64,256]{4,3,2,0,1:T(8,128)S(1)} %bitcast.258), channel_id=1, source_target_pairs={{0,32},{32,64},{64,96},{96,128},{128,160},{160,192},{192,224},{224... | collective-permute-start | bytes 2359304 | tf_op jit(solution)/shard_map/ppermute | solution.py:15
  11.5 22.1 %collective-permute-start.1 = (f32[3,1,4,64,256]{4,3,2,0,1:T(8,128)S(1)}, f32[3,1,4,64,256]{4,3,2,0,1:T(8,128)}, u32[]{:S(2)}, u32[]{:S(2)}) collective-permute-start(f32[3,1,4,64,256]{4,3,2,0,1:T(8,128)S(1)} %bitcast.259), channel_id=1, source_target_pairs={{32,0},{64,32},{96,64},{128,96},{160,128},{192,160},{224,192},{0,2... | collective-permute-start | bytes 2359304 | tf_op jit(solution)/shard_map/ppermute | solution.py:18
  15.6 19.9 %copy-start.18 = (s32[4]{0:T(128)}, s32[4]{0:T(128)S(1)}, u32[]{:S(2)}) copy-start(s32[4]{0:T(128)S(1)} %get-tuple-element.70) | copy-start | bytes 52
  18.8 230.9 %all-reduce.5.cloned.1.call-start = ((), (), s32[]{:S(2)}) async-start(), calls=%async_computation.3 | async-start | bytes 3145728 | tf_op jit(solution)/shard_map/psum | solution.py:91
  19.2 28.2 %copy-start.19 = (pred[4]{0:T(512)(128)(4,1)}, pred[4]{0:T(512)(128)(4,1)S(1)}, u32[]{:S(2)}) copy-start(pred[4]{0:T(512)(128)(4,1)S(1)} %compare_and_fusion.2) | copy-start | bytes 16
  19.3 29.6 %copy-start.20 = (pred[4]{0:T(512)(128)(4,1)}, pred[4]{0:T(512)(128)(4,1)S(1)}, u32[]{:S(2)}) copy-start(pred[4]{0:T(512)(128)(4,1)S(1)} %compare_and_fusion.4) | copy-start | bytes 16
  19.3 30.9 %copy-start.21 = (pred[4]{0:T(512)(128)(4,1)}, pred[4]{0:T(512)(128)(4,1)S(1)}, u32[]{:S(2)}) copy-start(pred[4]{0:T(512)(128)(4,1)S(1)} %compare_and_fusion.5) | copy-start | bytes 16
  19.3 31.1 %copy-start.22 = (pred[4]{0:T(512)(128)(4,1)}, pred[4]{0:T(512)(128)(4,1)S(1)}, u32[]{:S(2)}) copy-start(pred[4]{0:T(512)(128)(4,1)S(1)} %compare_and_fusion.6) | copy-start | bytes 16
  19.4 31.2 %copy-start.23 = (pred[4]{0:T(512)(128)(4,1)}, pred[4]{0:T(512)(128)(4,1)S(1)}, u32[]{:S(2)}) copy-start(pred[4]{0:T(512)(128)(4,1)S(1)} %compare_and_fusion.7) | copy-start | bytes 16
  19.4 31.4 %copy-start.24 = (pred[4]{0:T(512)(128)(4,1)}, pred[4]{0:T(512)(128)(4,1)S(1)}, u32[]{:S(2)}) copy-start(pred[4]{0:T(512)(128)(4,1)S(1)} %compare_and_fusion.8) | copy-start | bytes 16
  19.7 31.8 %copy-start.25 = (pred[4]{0:T(512)(128)(4,1)}, pred[4]{0:T(512)(128)(4,1)S(1)}, u32[]{:S(2)}) copy-start(pred[4]{0:T(512)(128)(4,1)S(1)} %compare_and_fusion.9) | copy-start | bytes 16
  19.8 32.1 %copy-start.26 = (pred[4]{0:T(512)(128)(4,1)}, pred[4]{0:T(512)(128)(4,1)S(1)}, u32[]{:S(2)}) copy-start(pred[4]{0:T(512)(128)(4,1)S(1)} %compare_and_fusion.3) | copy-start | bytes 16
  19.8 32.3 %copy-start.27 = (f32[4]{0:T(128)}, f32[4]{0:T(128)S(1)}, u32[]{:S(2)}) copy-start(f32[4]{0:T(128)S(1)} %broadcast_subtract_fusion) | copy-start | bytes 52
  47.5 2.8 copy-start.5
  47.5 3.0 copy-start.6
  48.9 1.7 copy-start.8
  55.3 3.9 %copy-start.33 = (s32[64]{0:T(128)S(1)}, s32[64]{0:T(128)}, u32[]{:S(2)}) copy-start(s32[64]{0:T(128)} %param.13) | copy-start | bytes 772
  55.4 5.0 %copy-start.32 = (s32[4]{0:T(128)S(1)}, s32[4]{0:T(128)}, u32[]{:S(2)}) copy-start(s32[4]{0:T(128)} %param.14) | copy-start | bytes 52
  112.2 142.2 %copy-start.3 = (f32[4,3,64,256]{3,2,1,0:T(8,128)S(1)}, f32[4,3,64,256]{3,2,1,0:T(8,128)}, u32[]{:S(2)}) copy-start(f32[4,3,64,256]{3,2,1,0:T(8,128)} %gather_fusion.7) | copy-start | bytes 2359300
  112.2 142.2 %copy-start.4 = (f32[4,3,64,256]{3,2,1,0:T(8,128)S(1)}, f32[4,3,64,256]{3,2,1,0:T(8,128)}, u32[]{:S(2)}) copy-start(f32[4,3,64,256]{3,2,1,0:T(8,128)} %gather_fusion.5) | copy-start | bytes 2359300
  249.7 4.7 %copy-start.7 = (f32[4,3,64,256]{3,2,1,0:T(8,128)S(1)}, f32[4,3,64,256]{3,2,1,0:T(8,128)}, u32[]{:S(2)}) copy-start(f32[4,3,64,256]{3,2,1,0:T(8,128)} %gather_fusion.3) | copy-start | bytes 2359300
  249.7 4.7 %copy-start.9 = (f32[4,3,64,256]{3,2,1,0:T(8,128)S(1)}, f32[4,3,64,256]{3,2,1,0:T(8,128)}, u32[]{:S(2)}) copy-start(f32[4,3,64,256]{3,2,1,0:T(8,128)} %gather_fusion.2) | copy-start | bytes 2359300
  249.7 4.7 %copy-start.11 = (f32[4,3,64,256]{3,2,1,0:T(8,128)S(1)}, f32[4,3,64,256]{3,2,1,0:T(8,128)}, u32[]{:S(2)}) copy-start(f32[4,3,64,256]{3,2,1,0:T(8,128)} %gather_fusion.1) | copy-start | bytes 2359300
  249.7 4.7 %copy-start.14 = (f32[3,1,4,64,128]{4,3,2,1,0:T(8,128)S(1)}, f32[3,1,4,64,128]{4,3,2,1,0:T(8,128)}, u32[]{:S(2)}) copy-start(f32[3,1,4,64,128]{4,3,2,1,0:T(8,128)} %param.10) | copy-start | bytes 1179652
  249.7 4.7 %copy-start.15 = (f32[4,64,256]{2,1,0:T(8,128)S(1)}, f32[4,64,256]{2,1,0:T(8,128)}, u32[]{:S(2)}) copy-start(f32[4,64,256]{2,1,0:T(8,128)} %get-tuple-element.40) | copy-start | bytes 786436
  296.2 20.6 %all-to-all-start.1 = ((f32[3,1,4,64,128]{4,2,0,1,3:T(4,128)}), f32[3,1,4,64,128]{4,2,0,1,3:T(4,128)S(1)}, u32[]{:S(2)}, u32[]{:S(2)}) async-start(f32[3,1,4,64,128]{4,2,0,1,3:T(4,128)} %reshape.459), calls=%async_computation.1 | async-start | bytes 786432 | tf_op jit(solution)/shard_map/all_to_all | solution.py:113
  (7 other events, 7.8 us)
Sparse Core Ops, SparseCore 0:
  18.9 76.5 all-reduce.2
  98.9 150.7 all-reduce.4
where the time goes:
time: 328 us; the launch traced here: 327 us
  waiting for transfers between devices  196 us (60%)
  local copies, waits for them, and re-layouts  50.8 us (15%)
  blocking collectives  27.5 us (8%)
  matrix products  17.6 us (5%)
  between operations  14.4 us (4%)
  starting transfers between devices  12.1 us (4%)
  other arithmetic  8.77 us (3%)
    psum x1, waiting for transfers between devices, local(): summed = lax.psum(stress, ('kx', 'real'))  134 us
    psum x1, waiting for transfers between devices, local(): low_fields = lax.psum(own_low, 'kx')  35.1 us
    all_to_all x1, blocking collectives, local(): lax.all_to_all(flat_out, ('kx', 'ht'), split_axis=3, concat_axis=3, tiled...  27.5 us
    all_to_all x1, waiting for transfers between devices, local(): lax.all_to_all(applied, ('kx', 'ht'), split_axis=3, concat_axis=3, tiled=...  14.2 us
    ppermute x1, waiting for transfers between devices, extended_2(): lax.ppermute(lax.slice_in_dim(block, block.shape[dim] - width, None, axis...  12.9 us
    gather x8, local copies, waits for them, and re-layouts, local(): partner = jnp.take(extended, local_partner[:, member], axis=2)  12 us
    unnamed x84, local copies, waits for them, and re-layouts  11.8 us
    slice x1, local copies, waits for them, and re-layouts, local(): low_one = low_fields[:, :, member:member + 1]  7.67 us
  transfers between devices with their start and end apart: 5, of which 4 were waited for; matrix products, arithmetic and copies ran while one was open for 15% of the time, Pallas kernels for 0%

commit v1 on v0

--- a/solution.py
+++ b/solution.py
@@ -77,7 +77,8 @@
     physical = jnp.dot(current, forward, precision=highest)
     extended = extended_2(physical, (("kx", 2),), band_modes)
     own_low = jnp.einsum("jm,crmyz->crjyz", low_select, physical, precision=highest)
-    low_fields = lax.psum(own_low, "kx")
+    parts = lax.all_gather(own_low, "kx", axis=0, tiled=False)
+    low_fields = parts.sum(axis=0)
     high_low = jnp.zeros_like(physical)
     stresses = []
     for member in range(low_members):

time: 328 us -> 391 us (1.19)
  waiting for transfers between devices: 196 us -> 265 us
  local copies, waits for them, and re-layouts: 50.8 us -> 41.9 us
  other arithmetic: 8.77 us -> 15.7 us
  matrix products: 17.6 us -> 11.5 us
    psum x1, waiting for transfers between devices: 134 us -> 236 us  [local(): summed = lax.psum(stress, ('kx', 'real'))]
    psum x1 -> x0, waiting for transfers between devices: 35.1 us -> none  [local(): low_fields = lax.psum(own_low, 'kx')]
    unnamed x84 -> x73, local copies, waits for them, and re-layouts: 11.8 us -> 4.87 us
    another operation x9, local copies, waits for them, and re-layouts: 4.95 us -> 11.7 us  [local(): stress = jnp.stack(stresses, axis=1)]
    slice x1, local copies, waits for them, and re-layouts: 7.67 us -> 1.45 us  [local(): low_one = low_fields[:, :, member:member + 1]]
    reduce_sum x0 -> x1, other arithmetic: none -> 6.1 us  [local(): low_fields = parts.sum(axis=0)]
  transfers between devices with their start and end apart: 5 -> 5, of which waited for: 4 -> 3; matrix products, arithmetic and copies ran while one was open for 15% -> 2% of each run, Pallas kernels for 0% -> 0%
where the time goes in v1:
time: 391 us; the launch traced here: 390 us
  waiting for transfers between devices  265 us (68%)
  local copies, waits for them, and re-layouts  41.9 us (11%)
  blocking collectives  27.5 us (7%)
  between operations  15.8 us (4%)
  other arithmetic  15.7 us (4%)
  starting transfers between devices  12.2 us (3%)
  matrix products  11.5 us (3%)
    psum x1, waiting for transfers between devices, local(): summed = lax.psum(stress, ('kx', 'real'))  236 us
    all_to_all x1, blocking collectives, local(): lax.all_to_all(flat_out, ('kx', 'ht'), split_axis=3, concat_axis=3, tiled...  27.5 us
    ppermute x1, waiting for transfers between devices, extended_2(): lax.ppermute(lax.slice_in_dim(block, block.shape[dim] - width, None, axis...  14.9 us
    all_to_all x1, waiting for transfers between devices, local(): lax.all_to_all(applied, ('kx', 'ht'), split_axis=3, concat_axis=3, tiled=...  14.3 us
    gather x8, local copies, waits for them, and re-layouts, local(): partner = jnp.take(extended, local_partner[:, member], axis=2)  12 us
    another operation x9, local copies, waits for them, and re-layouts, local(): stress = jnp.stack(stresses, axis=1)  11.7 us
  transfers between devices with their start and end apart: 5, of which 3 were waited for; matrix products, arithmetic and copies ran while one was open for 2% of the time, Pallas kernels for 0%

profile of v1, /device:TPU:1, one launch (start us, length us, event | category | flops | bytes accessed | tf_op | source)
XLA Modules:
  0.0 389.8 jit_solution(3383357565651062778)
XLA Ops:
  7.4 2.4 fusion.12
  9.8 2.5 collective-permute-start
  12.4 4.0 %collective-permute-start.1 = (f32[3,1,4,64,256]{4,3,2,0,1:T(8,128)S(1)}, f32[3,1,4,64,256]{4,3,2,0,1:T(8,128)}, u32[]{:S(2)}, u32[]{:S(2)}) collective-permute-start(f32[3,1,4,64,256]{4,3,2,0,1:T(8,128)S(1)} %bitcast.266), channel_id=1, source_target_pairs={{32,0},{64,32},{96,64},{128,96},{160,128},{192,160},{224,192},{0,2... | collective-permute-start | bytes 2359304 | tf_op jit(solution)/shard_map/ppermute | solution.py:18
  18.6 14.9 %collective-permute-done = f32[3,1,4,64,256]{4,3,2,0,1:T(8,128)S(1)} collective-permute-done((f32[3,1,4,64,256]{4,3,2,0,1:T(8,128)S(1)}, f32[3,1,4,64,256]{4,3,2,0,1:T(8,128)S(1)}, u32[]{:S(2)}, u32[]{:S(2)}) %collective-permute-start) | collective-permute-done | bytes 786464 | tf_op jit(solution)/shard_map/ppermute | solution.py:15
  34.4 1.8 maximum_bitcast_fusion
  36.2 1.5 gather_fusion.7
  37.8 1.5 gather_fusion.5
  39.3 1.5 gather_fusion.4
  40.7 1.5 gather_fusion.3
  42.2 1.5 gather_fusion.2
  43.7 1.5 gather_fusion.1
  45.2 1.5 gather_fusion
  46.7 1.5 gather_fusion.6
  48.2 1.4 bitcast_select_fusion.2
  49.6 1.3 bitcast_select_fusion.4
  52.8 1.4 multiply_bitcast_fusion.1
  61.3 5.2 %stack.35 = f32[3,8,64,256]{3,1,2,0:T(8,128)} concatenate(f32[3,1,64,256]{3,1,2,0:T(1,128)} %stack.27, f32[3,1,64,256]{3,1,2,0:T(1,128)} %stack.28, f32[3,1,64,256]{3,1,2,0:T(1,128)} %stack.29, f32[3,1,64,256]{3,1,2,0:T(1,128)} %stack.30, f32[3,1,64,256]{3,1,2,0:T(1,128)} %stack.31, f32[3,1,64,256]{3,1,2,0:T(1,128)} %stack.32, f32[3,1,64,256]{3,1,2,0:T(1,128)} %stack.33, ...), dimensions={1} | concatenate | bytes 3145728 | tf_op jit(solution)/shard_map/stack | solution.py:90
  66.8 1.3 convolution_bitcast_fusion
  68.2 1.6 copy.35
  70.0 235.8 %all-reduce.2.cloned.1.call-done = f32[3,8,64,256]{3,1,2,0:T(8,128)} async-done(((f32[3,8,64,256]{3,1,2,0:T(8,128)}), f32[3,8,64,256]{3,1,2,0:T(8,128)}) %all-reduce.2.cloned.1.call-update) | async-done | bytes 1572880 | tf_op jit(solution)/shard_map/psum | solution.py:92
  305.8 3.3 fusion
  309.7 6.1 %bitcast_reduce_fusion = f32[3,8,64,256]{3,2,1,0:T(8,128)S(1)} fusion(f32[8,3,8,64,256]{4,3,2,1,0:T(8,128)} %bitcast.264), kind=kLoop, calls=%fused_computation.11 | loop fusion | flops 2752512 | bytes 14155776 | tf_op jit(solution)/shard_map/reduce_sum | solution.py:81
  316.8 1.5 fusion.51
  320.8 2.4 fusion.6
  324.0 1.3 gather_fusion.8
  326.5 27.5 %all_to_all.10 = f32[3,1,4,64,128]{4,2,0,1,3:T(4,128)S(1)} all-to-all(f32[3,1,4,64,128]{4,2,0,1,3:T(4,128)S(1)} %reshape.460), channel_id=1, replica_groups=mesh['kx'=8,'ht'=8,'real'=4] {'kx','ht'}, dimensions={3} | all-to-all | bytes 786432 | tf_op jit(solution)/shard_map/all_to_all | solution.py:107
  354.9 1.5 convolution_bitcast_fusion.1
  357.0 1.3 reshape.462
  358.3 5.4 %all-to-all-start.1 = ((f32[3,1,4,64,128]{4,2,0,1,3:T(4,128)}), f32[3,1,4,64,128]{4,2,0,1,3:T(4,128)S(1)}, u32[]{:S(2)}, u32[]{:S(2)}) async-start(f32[3,1,4,64,128]{4,2,0,1,3:T(4,128)} %reshape.462), calls=%async_computation.1 | async-start | bytes 786432 | tf_op jit(solution)/shard_map/all_to_all | solution.py:114
  364.6 14.3 %all-to-all-done.1 = f32[3,1,4,64,128]{4,2,0,1,3:T(4,128)S(1)} async-done(((f32[3,1,4,64,128]{4,2,0,1,3:T(4,128)}), f32[3,1,4,64,128]{4,2,0,1,3:T(4,128)S(1)}, u32[]{:S(2)}, u32[]{:S(2)}) %all-to-all-start.1) | async-done | bytes 393248 | tf_op jit(solution)/shard_map/all_to_all | solution.py:114
  379.7 1.1 gather_fusion.9
  381.4 1.0 copy.51
  (152 shorter events, 21.5 us)
Async XLA Ops:
  7.4 347.5 %copy-start = (f32[1,512,512]{2,1,0:T(8,128)S(1)}, f32[1,512,512]{2,1,0:T(8,128)}, u32[]{:S(2)}) copy-start(f32[1,512,512]{2,1,0:T(8,128)} %param.15) | copy-start | bytes 3145732
  7.4 298.4 %all-reduce.2.cloned.1.call-start = ((), (), s32[]{:S(2)}) async-start(), calls=%async_computation.2 | async-start | bytes 3145728 | tf_op jit(solution)/shard_map/psum | solution.py:92
  9.8 23.7 %copy-start.1 = (f32[256,3,4,64]{0,3,2,1:T(8,128)}, f32[256,3,4,64]{0,3,2,1:T(8,128)S(1)}, u32[]{:S(2)}) copy-start(f32[256,3,4,64]{0,3,2,1:T(8,128)S(1)} %fusion.12) | copy-start | bytes 2359300
  9.8 23.7 %collective-permute-start = (f32[3,1,4,64,256]{4,3,2,0,1:T(8,128)S(1)}, f32[3,1,4,64,256]{4,3,2,0,1:T(8,128)S(1)}, u32[]{:S(2)}, u32[]{:S(2)}) collective-permute-start(f32[3,1,4,64,256]{4,3,2,0,1:T(8,128)S(1)} %bitcast.265), channel_id=1, source_target_pairs={{0,32},{32,64},{64,96},{96,128},{128,160},{160,192},{192,224},{224... | collective-permute-start | bytes 2359304 | tf_op jit(solution)/shard_map/ppermute | solution.py:15
  12.4 22.1 %collective-permute-start.1 = (f32[3,1,4,64,256]{4,3,2,0,1:T(8,128)S(1)}, f32[3,1,4,64,256]{4,3,2,0,1:T(8,128)}, u32[]{:S(2)}, u32[]{:S(2)}) collective-permute-start(f32[3,1,4,64,256]{4,3,2,0,1:T(8,128)S(1)} %bitcast.266), channel_id=1, source_target_pairs={{32,0},{64,32},{96,64},{128,96},{160,128},{192,160},{224,192},{0,2... | collective-permute-start | bytes 2359304 | tf_op jit(solution)/shard_map/ppermute | solution.py:18
  48.2 2.8 copy-start.5
  48.2 2.9 copy-start.6
  49.6 1.7 copy-start.7
  51.0 1.1 copy-start.9
  51.1 1.2 copy-start.11
  51.3 1.3 copy-start.13
  52.8 1.6 copy-start.2
  61.3 5.5 %copy-start.25 = (s32[8]{0:T(128)S(1)}, s32[8]{0:T(128)}, u32[]{:S(2)}) copy-start(s32[8]{0:T(128)} %param.11) | copy-start | bytes 100
  66.6 243.1 %all-gather.3.cloned.1.call-start = ((), (), s32[]{:S(2)}) async-start(), calls=%async_computation.3 | async-start | bytes 14155776 | tf_op jit(solution)/shard_map/all_gather | solution.py:80
  68.2 1.7 copy-start.27
  68.2 1.7 copy-start.26
  316.7 2.3 copy-start.16
  316.7 2.3 copy-start.17
  316.7 2.3 copy-start.18
  316.7 2.3 copy-start.19
  316.7 2.3 copy-start.20
  316.8 2.3 copy-start.21
  316.8 2.3 copy-start.22
  316.8 2.3 copy-start.23
  318.2 1.1 copy-start.14
  318.3 1.2 copy-start.15
  318.6 1.2 copy-start.3
  318.6 1.4 copy-start.4
  318.7 1.7 copy-start.8
  318.7 1.9 copy-start.10
  318.7 2.1 copy-start.12
  358.3 20.6 %all-to-all-start.1 = ((f32[3,1,4,64,128]{4,2,0,1,3:T(4,128)}), f32[3,1,4,64,128]{4,2,0,1,3:T(4,128)S(1)}, u32[]{:S(2)}, u32[]{:S(2)}) async-start(f32[3,1,4,64,128]{4,2,0,1,3:T(4,128)} %reshape.462), calls=%async_computation.1 | async-start | bytes 786432 | tf_op jit(solution)/shard_map/all_to_all | solution.py:114
  (1 other events, 0.9 us)
Sparse Core Ops, SparseCore 0:
  66.7 239.0 all-reduce.1
Sparse Core Ops, SparseCore 1:
  69.9 142.2 all-gather.2
